TPU v7x, 256 devices: a whole 4x4x8 slice. The times are simulated.
256 devices in a mesh: row: 16 (over z_hi, y, core), col: 16 (over x, z_lo).
Axes of the slice: x: 4, y: 4, z: 8 (z_hi: 2, z_lo: 4; z = z_hi * 4 + z_lo), core: 2. Of those that a mesh axis runs over, the one named last changes fastest.
Arguments:
- act_sketch: bfloat16 [2, 8192, 256], P(None, 'row'), may hold values from -6 to 6
- grad_sketch: bfloat16 [2, 8192, 256], P(None, 'row'), may hold values from -6 to 6
- targets: float32 [8192, 256], P('row'), may hold values from -6 to 6
Outputs:
- residual: float32 [8192, 256], P(('row', 'col'))
All inputs are finite; a program needn't handle non-finite values.
Results may differ from a plain program's by a relative error of at most 0.014.
The roundings to bfloat16 on the way count: a program that leaves them out, or rounds other values in their place, can miss the bound.
Values may be sent and summed in bfloat16 or wider, within the bound.
A program may use at most 64 MiB of HBM per device.

v0:
```python
import math
import jax
import jax.numpy as jnp
from jax import lax
from jax.sharding import PartitionSpec as P

ITERS = 8


def broadcast(value, axis, source):
    kept = jnp.where(lax.axis_index(axis) == source, value, 0).astype(value.dtype)
    return lax.psum(kept, axis)


def spread(panel, root):
    return broadcast(panel, "row", root)


def gram_pair(left, right):
    return lax.dot_general(
        left, right, (((1,), (1,)), ((), ())), preferred_element_type=jnp.float32
    )


def body(act_sketch, grad_sketch, targets):
    row_count = lax.axis_size("row")
    col_count = lax.axis_size("col")
    ratio = col_count // row_count
    examples = targets.shape[0]
    col_block = examples // ratio
    share_rows = examples // col_count
    col_place = lax.axis_index("col")
    root = col_place // ratio
    scale = act_sketch.shape[2] * math.sqrt(examples * row_count) / 4.0
    act_cols, grad_cols = (broadcast(act_sketch, "row", root), broadcast(grad_sketch, "row", root))
    total = jnp.zeros((examples, col_block), jnp.float32)
    for layer in range(act_sketch.shape[0]):
        act_gram = gram_pair(act_sketch[layer], act_cols[layer])
        grad_gram = gram_pair(grad_sketch[layer], grad_cols[layer])
        total = total + act_gram * grad_gram
    kernel = (total / scale).astype(jnp.bfloat16)
    share = lax.dynamic_slice_in_dim(targets, col_place * share_rows, share_rows, 0)
    for step in range(ITERS):
        squashed = jnp.tanh(share).astype(jnp.bfloat16)
        gathered = lax.all_gather(squashed, "col", axis=0, tiled=True)
        panel = spread(gathered, root)
        partial_value = jnp.dot(kernel, panel, preferred_element_type=jnp.float32)
        piece = lax.psum_scatter(partial_value, "col", scatter_dimension=0, tiled=True)
        share = share - 0.05 * piece
    return share


def solution(mesh):
    return jax.shard_map(
        body,
        mesh=mesh,
        in_specs=(P(None, "row", None), P(None, "row", None), P("row", None)),
        out_specs=P(("row", "col"), None),
        check_vma=False,
    )
```

profile of v0, /device:TPU:8, one launch (start us, length us, event | category | flops | bytes accessed | tf_op | source)
XLA Modules:
  0.0 2479.9 jit_solution(18417355909062240451)
XLA Ops:
  7.4 46.0 %all_gather.24 = bf16[512,256]{1,0:T(8,128)(2,1)S(1)} all-gather(bf16[32,256]{1,0:T(8,128)(2,1)S(1)} %tanh_convert_fusion.7), channel_id=1, replica_groups=mesh['row'=16,'col'=16] {'col'}, dimensions={0}, use_global_device_ids=true | all-gather | bytes 278528 | tf_op jit(solution)/shard_map/all_gather | solution.py:45
  55.2 172.0 %all-reduce.24.cloned.1.call-done = (bf16[2,512,256]{2,1,0:T(8,128)(2,1)}, bf16[2,512,256]{2,1,0:T(8,128)(2,1)}, bf16[512,256]{1,0:T(8,128)(2,1)}) async-done(((bf16[2,512,256]{2,1,0:T(8,128)(2,1)}, bf16[2,512,256]{2,1,0:T(8,128)(2,1)}, bf16[512,256]{1,0:T(8,128)(2,1)}), (bf16[2,512,256]{2,1,0:T(8,128)(2,1)}, bf16[2,512,256]{2,1,0:T(8,128)(2,1)}, bf16[512,256]{1,0:T(8,128)(2,1)})) %all-reduce.24.cloned.1.call-update) | async-done | bytes 1310736 | tf_op jit(solution)/shard_map/psum | solution.py:12
  232.1 94.1 %reduce-scatter.9.cloned.1.call-done = f32[32,256]{1,0:T(8,128)} async-done(((f32[512,256]{1,0:T(8,128)}), f32[32,256]{1,0:T(8,128)}) %reduce-scatter.9.cloned.1.call-update) | async-done | bytes 32784 | tf_op jit(solution)/shard_map/reduce_scatter | solution.py:48
  327.0 39.1 %all_gather.25 = bf16[512,256]{1,0:T(8,128)(2,1)S(1)} all-gather(bf16[32,256]{1,0:T(8,128)(2,1)S(1)} %get-tuple-element.12), channel_id=1, replica_groups=mesh['row'=16,'col'=16] {'col'}, dimensions={0}, use_global_device_ids=true | all-gather | bytes 278528 | tf_op jit(solution)/shard_map/all_gather | solution.py:45
  367.0 169.6 %all-reduce.10.cloned.1.call-done = bf16[512,256]{1,0:T(8,128)(2,1)} async-done(((bf16[512,256]{1,0:T(8,128)(2,1)}), bf16[512,256]{1,0:T(8,128)(2,1)}) %all-reduce.10.cloned.1.call-update) | async-done | bytes 262160 | tf_op jit(solution)/shard_map/psum | solution.py:12
  538.7 94.2 %reduce-scatter.11.cloned.1.call-done = f32[32,256]{1,0:T(8,128)} async-done(((f32[512,256]{1,0:T(8,128)}), f32[32,256]{1,0:T(8,128)}) %reduce-scatter.11.cloned.1.call-update) | async-done | bytes 32784 | tf_op jit(solution)/shard_map/reduce_scatter | solution.py:48
  633.8 39.5 %all_gather.26 = bf16[512,256]{1,0:T(8,128)(2,1)S(1)} all-gather(bf16[32,256]{1,0:T(8,128)(2,1)S(1)} %tanh_convert_fusion.5), channel_id=1, replica_groups=mesh['row'=16,'col'=16] {'col'}, dimensions={0}, use_global_device_ids=true | all-gather | bytes 278528 | tf_op jit(solution)/shard_map/all_gather | solution.py:45
  674.0 169.0 %all-reduce.12.cloned.1.call-done = bf16[512,256]{1,0:T(8,128)(2,1)} async-done(((bf16[512,256]{1,0:T(8,128)(2,1)}), bf16[512,256]{1,0:T(8,128)(2,1)}) %all-reduce.12.cloned.1.call-update) | async-done | bytes 262160 | tf_op jit(solution)/shard_map/psum | solution.py:12
  845.2 94.2 %reduce-scatter.13.cloned.1.call-done = f32[32,256]{1,0:T(8,128)} async-done(((f32[512,256]{1,0:T(8,128)}), f32[32,256]{1,0:T(8,128)}) %reduce-scatter.13.cloned.1.call-update) | async-done | bytes 32784 | tf_op jit(solution)/shard_map/reduce_scatter | solution.py:48
  940.2 39.5 %all_gather.27 = bf16[512,256]{1,0:T(8,128)(2,1)S(1)} all-gather(bf16[32,256]{1,0:T(8,128)(2,1)S(1)} %get-tuple-element.10), channel_id=1, replica_groups=mesh['row'=16,'col'=16] {'col'}, dimensions={0}, use_global_device_ids=true | all-gather | bytes 278528 | tf_op jit(solution)/shard_map/all_gather | solution.py:45
  980.5 169.0 %all-reduce.14.cloned.1.call-done = bf16[512,256]{1,0:T(8,128)(2,1)} async-done(((bf16[512,256]{1,0:T(8,128)(2,1)}), bf16[512,256]{1,0:T(8,128)(2,1)}) %all-reduce.14.cloned.1.call-update) | async-done | bytes 262160 | tf_op jit(solution)/shard_map/psum | solution.py:12
  1151.6 94.4 %reduce-scatter.15.cloned.1.call-done = f32[32,256]{1,0:T(8,128)} async-done(((f32[512,256]{1,0:T(8,128)}), f32[32,256]{1,0:T(8,128)}) %reduce-scatter.15.cloned.1.call-update) | async-done | bytes 32784 | tf_op jit(solution)/shard_map/reduce_scatter | solution.py:48
  1246.8 39.5 %all_gather.28 = bf16[512,256]{1,0:T(8,128)(2,1)S(1)} all-gather(bf16[32,256]{1,0:T(8,128)(2,1)S(1)} %tanh_convert_fusion.3), channel_id=1, replica_groups=mesh['row'=16,'col'=16] {'col'}, dimensions={0}, use_global_device_ids=true | all-gather | bytes 278528 | tf_op jit(solution)/shard_map/all_gather | solution.py:45
  1287.1 169.2 %all-reduce.16.cloned.1.call-done = bf16[512,256]{1,0:T(8,128)(2,1)} async-done(((bf16[512,256]{1,0:T(8,128)(2,1)}), bf16[512,256]{1,0:T(8,128)(2,1)}) %all-reduce.16.cloned.1.call-update) | async-done | bytes 262160 | tf_op jit(solution)/shard_map/psum | solution.py:12
  1458.5 94.2 %reduce-scatter.17.cloned.1.call-done = f32[32,256]{1,0:T(8,128)} async-done(((f32[512,256]{1,0:T(8,128)}), f32[32,256]{1,0:T(8,128)}) %reduce-scatter.17.cloned.1.call-update) | async-done | bytes 32784 | tf_op jit(solution)/shard_map/reduce_scatter | solution.py:48
  1553.5 39.5 %all_gather.29 = bf16[512,256]{1,0:T(8,128)(2,1)S(1)} all-gather(bf16[32,256]{1,0:T(8,128)(2,1)S(1)} %get-tuple-element.8), channel_id=1, replica_groups=mesh['row'=16,'col'=16] {'col'}, dimensions={0}, use_global_device_ids=true | all-gather | bytes 278528 | tf_op jit(solution)/shard_map/all_gather | solution.py:45
  1593.7 169.0 %all-reduce.18.cloned.1.call-done = bf16[512,256]{1,0:T(8,128)(2,1)} async-done(((bf16[512,256]{1,0:T(8,128)(2,1)}), bf16[512,256]{1,0:T(8,128)(2,1)}) %all-reduce.18.cloned.1.call-update) | async-done | bytes 262160 | tf_op jit(solution)/shard_map/psum | solution.py:12
  1764.9 94.2 %reduce-scatter.19.cloned.1.call-done = f32[32,256]{1,0:T(8,128)} async-done(((f32[512,256]{1,0:T(8,128)}), f32[32,256]{1,0:T(8,128)}) %reduce-scatter.19.cloned.1.call-update) | async-done | bytes 32784 | tf_op jit(solution)/shard_map/reduce_scatter | solution.py:48
  1859.9 39.5 %all_gather.30 = bf16[512,256]{1,0:T(8,128)(2,1)S(1)} all-gather(bf16[32,256]{1,0:T(8,128)(2,1)S(1)} %tanh_convert_fusion.1), channel_id=1, replica_groups=mesh['row'=16,'col'=16] {'col'}, dimensions={0}, use_global_device_ids=true | all-gather | bytes 278528 | tf_op jit(solution)/shard_map/all_gather | solution.py:45
  1900.2 169.0 %all-reduce.20.cloned.1.call-done = bf16[512,256]{1,0:T(8,128)(2,1)} async-done(((bf16[512,256]{1,0:T(8,128)(2,1)}), bf16[512,256]{1,0:T(8,128)(2,1)}) %all-reduce.20.cloned.1.call-update) | async-done | bytes 262160 | tf_op jit(solution)/shard_map/psum | solution.py:12
  2071.4 94.2 %reduce-scatter.21.cloned.1.call-done = f32[32,256]{1,0:T(8,128)} async-done(((f32[512,256]{1,0:T(8,128)}), f32[32,256]{1,0:T(8,128)}) %reduce-scatter.21.cloned.1.call-update) | async-done | bytes 32784 | tf_op jit(solution)/shard_map/reduce_scatter | solution.py:48
  2166.4 39.5 %all_gather.31 = bf16[512,256]{1,0:T(8,128)(2,1)S(1)} all-gather(bf16[32,256]{1,0:T(8,128)(2,1)S(1)} %tanh_convert_fusion), channel_id=1, replica_groups=mesh['row'=16,'col'=16] {'col'}, dimensions={0}, use_global_device_ids=true | all-gather | bytes 278528 | tf_op jit(solution)/shard_map/all_gather | solution.py:45
  2206.6 169.0 %all-reduce.22.cloned.1.call-done = bf16[512,256]{1,0:T(8,128)(2,1)} async-done(((bf16[512,256]{1,0:T(8,128)(2,1)}), bf16[512,256]{1,0:T(8,128)(2,1)}) %all-reduce.22.cloned.1.call-update) | async-done | bytes 262160 | tf_op jit(solution)/shard_map/psum | solution.py:12
  2377.8 94.2 %reduce-scatter.23.cloned.1.call-done = f32[32,256]{1,0:T(8,128)} async-done(((f32[512,256]{1,0:T(8,128)}), f32[32,256]{1,0:T(8,128)}) %reduce-scatter.23.cloned.1.call-update) | async-done | bytes 32784 | tf_op jit(solution)/shard_map/reduce_scatter | solution.py:48
  (80 shorter events, 34.7 us)
Async XLA Ops:
  6.5 47.5 %copy-start = (bf16[2,512,256]{2,1,0:T(8,128)(2,1)S(1)}, bf16[2,512,256]{2,1,0:T(8,128)(2,1)}, u32[]{:S(2)}) copy-start(bf16[2,512,256]{2,1,0:T(8,128)(2,1)} %param.4) | copy-start | bytes 1572868
  6.5 220.7 %all-reduce.24.cloned.1.call-start = ((), (), s32[]{:S(2)}) async-start(), calls=%async_computation.23 | async-start | bytes 2621440 | tf_op jit(solution)/shard_map/psum | solution.py:12
  55.1 172.1 %copy-start.1 = (bf16[2,512,256]{2,1,0:T(8,128)(2,1)S(1)}, bf16[2,512,256]{2,1,0:T(8,128)(2,1)}, u32[]{:S(2)}) copy-start(bf16[2,512,256]{2,1,0:T(8,128)(2,1)} %param.3) | copy-start | bytes 1572868
  55.1 271.1 %reduce-scatter.9.cloned.1.call-start = ((), (), s32[]{:S(2)}) async-start(), calls=%async_computation.8 | async-start | bytes 557056 | tf_op jit(solution)/shard_map/reduce_scatter | solution.py:48
  227.2 1.4 copy-start.3
  228.6 1.0 copy-start.2
  232.1 304.5 %all-reduce.10.cloned.1.call-start = ((), (), s32[]{:S(2)}) async-start(), calls=%async_computation.9 | async-start | bytes 524288 | tf_op jit(solution)/shard_map/psum | solution.py:12
  366.9 266.1 %reduce-scatter.11.cloned.1.call-start = ((), (), s32[]{:S(2)}) async-start(), calls=%async_computation.10 | async-start | bytes 557056 | tf_op jit(solution)/shard_map/reduce_scatter | solution.py:48
  538.7 304.3 %all-reduce.12.cloned.1.call-start = ((), (), s32[]{:S(2)}) async-start(), calls=%async_computation.11 | async-start | bytes 524288 | tf_op jit(solution)/shard_map/psum | solution.py:12
  674.0 265.5 %reduce-scatter.13.cloned.1.call-start = ((), (), s32[]{:S(2)}) async-start(), calls=%async_computation.12 | async-start | bytes 557056 | tf_op jit(solution)/shard_map/reduce_scatter | solution.py:48
  845.1 94.3 %copy-start.7 = (f32[32,256]{1,0:T(8,128)S(1)}, f32[32,256]{1,0:T(8,128)}, u32[]{:S(2)}) copy-start(f32[32,256]{1,0:T(8,128)} %reduce-scatter.11.cloned.1.call-done) | copy-start | bytes 98308
  845.1 304.4 %all-reduce.14.cloned.1.call-start = ((), (), s32[]{:S(2)}) async-start(), calls=%async_computation.13 | async-start | bytes 524288 | tf_op jit(solution)/shard_map/psum | solution.py:12
  980.4 265.6 %reduce-scatter.15.cloned.1.call-start = ((), (), s32[]{:S(2)}) async-start(), calls=%async_computation.14 | async-start | bytes 557056 | tf_op jit(solution)/shard_map/reduce_scatter | solution.py:48
  1151.6 304.7 %all-reduce.16.cloned.1.call-start = ((), (), s32[]{:S(2)}) async-start(), calls=%async_computation.15 | async-start | bytes 524288 | tf_op jit(solution)/shard_map/psum | solution.py:12
  1287.1 265.7 %reduce-scatter.17.cloned.1.call-start = ((), (), s32[]{:S(2)}) async-start(), calls=%async_computation.16 | async-start | bytes 557056 | tf_op jit(solution)/shard_map/reduce_scatter | solution.py:48
  1458.4 94.3 %copy-start.8 = (f32[32,256]{1,0:T(8,128)S(1)}, f32[32,256]{1,0:T(8,128)}, u32[]{:S(2)}) copy-start(f32[32,256]{1,0:T(8,128)} %reduce-scatter.15.cloned.1.call-done) | copy-start | bytes 98308
  1458.4 304.3 %all-reduce.18.cloned.1.call-start = ((), (), s32[]{:S(2)}) async-start(), calls=%async_computation.17 | async-start | bytes 524288 | tf_op jit(solution)/shard_map/psum | solution.py:12
  1593.7 265.5 %reduce-scatter.19.cloned.1.call-start = ((), (), s32[]{:S(2)}) async-start(), calls=%async_computation.18 | async-start | bytes 557056 | tf_op jit(solution)/shard_map/reduce_scatter | solution.py:48
  1764.9 304.3 %all-reduce.20.cloned.1.call-start = ((), (), s32[]{:S(2)}) async-start(), calls=%async_computation.19 | async-start | bytes 524288 | tf_op jit(solution)/shard_map/psum | solution.py:12
  1900.1 265.5 %reduce-scatter.21.cloned.1.call-start = ((), (), s32[]{:S(2)}) async-start(), calls=%async_computation.20 | async-start | bytes 557056 | tf_op jit(solution)/shard_map/reduce_scatter | solution.py:48
  2071.3 94.3 %copy-start.4 = (f32[32,256]{1,0:T(8,128)S(1)}, f32[32,256]{1,0:T(8,128)}, u32[]{:S(2)}) copy-start(f32[32,256]{1,0:T(8,128)} %reduce-scatter.19.cloned.1.call-done) | copy-start | bytes 98308
  2071.3 304.3 %all-reduce.22.cloned.1.call-start = ((), (), s32[]{:S(2)}) async-start(), calls=%async_computation.21 | async-start | bytes 524288 | tf_op jit(solution)/shard_map/psum | solution.py:12
  2206.6 265.4 %reduce-scatter.23.cloned.1.call-start = ((), (), s32[]{:S(2)}) async-start(), calls=%async_computation.22 | async-start | bytes 557056 | tf_op jit(solution)/shard_map/reduce_scatter | solution.py:48
  2377.7 94.2 %copy-start.6 = (f32[32,256]{1,0:T(8,128)S(1)}, f32[32,256]{1,0:T(8,128)}, u32[]{:S(2)}) copy-start(f32[32,256]{1,0:T(8,128)} %reduce-scatter.21.cloned.1.call-done) | copy-start | bytes 98308
  (1 other events, 1.0 us)
Sparse Core Ops, SparseCore 0:
  55.3 171.9 all-reduce.23
  232.2 93.9 reduce-scatter.8
  367.0 169.5 all-reduce.9
  538.9 93.9 reduce-scatter.10
  674.1 168.9 all-reduce.11
  845.4 93.9 reduce-scatter.12
  980.5 168.9 all-reduce.13
  1152.0 94.0 reduce-scatter.14
  1287.2 169.1 all-reduce.15
  1458.7 93.9 reduce-scatter.16
  1593.8 168.9 all-reduce.17
  1765.1 93.9 reduce-scatter.18
  1900.3 168.9 all-reduce.19
  2071.6 93.9 reduce-scatter.20
  2206.7 168.9 all-reduce.21
  2378.0 93.9 reduce-scatter.22
where the time goes:
time: 2480 us
  waiting for transfers between devices  2110 us (85%)
  blocking collectives  322 us (13%)
    psum x8, waiting for transfers between devices, broadcast(): return lax.psum(kept, axis)  1360 us
    reduce_scatter x8, waiting for transfers between devices, body(): lax.psum_scatter(partial_value, 'col', scatter_dimension=0, tiled=True)  754 us
    all_gather x8, blocking collectives, body(): gathered = lax.all_gather(squashed, 'col', axis=0, tiled=True)  322 us
  transfers between devices with their start and end apart: 16, of which 16 were waited for; matrix products, arithmetic and copies ran while one was open for 0% of the time, Pallas kernels for 0%

commit v1 on v0

--- a/solution.py
+++ b/solution.py
@@ -42,7 +42,9 @@
     share = lax.dynamic_slice_in_dim(targets, col_place * share_rows, share_rows, 0)
     for step in range(ITERS):
         squashed = jnp.tanh(share).astype(jnp.bfloat16)
-        gathered = lax.all_gather(squashed, "col", axis=0, tiled=True)
+        gathered = jnp.concatenate(
+            lax.all_to_all(jnp.stack([squashed] * lax.axis_size("col")), "col", 0, 0), axis=0
+        )
         panel = spread(gathered, root)
         partial_value = jnp.dot(kernel, panel, preferred_element_type=jnp.float32)
         piece = lax.psum_scatter(partial_value, "col", scatter_dimension=0, tiled=True)

time: 2480 us -> 2260 us (0.911)
  blocking collectives: 322 us -> 82.2 us
    all_gather x8 -> x0, blocking collectives: 322 us -> none  [body(): gathered = lax.all_gather(squashed, 'col', axis=0, tiled=True)]
    all_to_all x0 -> x7, blocking collectives: none -> 82.2 us  [body(): lax.all_to_all(jnp.stack([squashed] * lax.axis_size('col')), 'col', 0, 0)]
  transfers between devices with their start and end apart: 16 -> 17, of which waited for: 16 -> 17; matrix products, arithmetic and copies ran while one was open for 0% -> 0% of each run, Pallas kernels for 0% -> 0%
where the time goes in v1:
time: 2260 us
  waiting for transfers between devices  2120 us (94%)
  blocking collectives  82.2 us (4%)
    psum x8, waiting for transfers between devices, broadcast(): return lax.psum(kept, axis)  1360 us
    reduce_scatter x8, waiting for transfers between devices, body(): lax.psum_scatter(partial_value, 'col', scatter_dimension=0, tiled=True)  754 us
    all_to_all x7, blocking collectives, body(): lax.all_to_all(jnp.stack([squashed] * lax.axis_size('col')), 'col', 0, 0)  82.2 us
  transfers between devices with their start and end apart: 17, of which 17 were waited for; matrix products, arithmetic and copies ran while one was open for 0% of the time, Pallas kernels for 0%

profile of v1, /device:TPU:8, one launch (start us, length us, event | category | flops | bytes accessed | tf_op | source)
XLA Modules:
  0.0 2259.5 jit_solution(14603944613635490401)
XLA Ops:
  17.7 9.7 all-to-all-done
  28.3 172.4 %all-reduce.24.cloned.1.call-done = (bf16[2,512,256]{2,1,0:T(8,128)(2,1)}, bf16[2,512,256]{2,1,0:T(8,128)(2,1)}, bf16[512,256]{1,0:T(8,128)(2,1)}) async-done(((bf16[2,512,256]{2,1,0:T(8,128)(2,1)}, bf16[2,512,256]{2,1,0:T(8,128)(2,1)}, bf16[512,256]{1,0:T(8,128)(2,1)}), (bf16[2,512,256]{2,1,0:T(8,128)(2,1)}, bf16[2,512,256]{2,1,0:T(8,128)(2,1)}, bf16[512,256]{1,0:T(8,128)(2,1)})) %all-reduce.24.cloned.1.call-update) | async-done | bytes 1310736 | tf_op jit(solution)/shard_map/psum | solution.py:12
  205.6 94.1 %reduce-scatter.9.cloned.1.call-done = f32[32,256]{1,0:T(8,128)} async-done(((f32[512,256]{1,0:T(8,128)}), f32[32,256]{1,0:T(8,128)}) %reduce-scatter.9.cloned.1.call-update) | async-done | bytes 32784 | tf_op jit(solution)/shard_map/reduce_scatter | solution.py:50
  300.5 11.7 all_to_all.40
  313.1 169.1 %all-reduce.10.cloned.1.call-done = bf16[512,256]{1,0:T(8,128)(2,1)} async-done(((bf16[512,256]{1,0:T(8,128)(2,1)}), bf16[512,256]{1,0:T(8,128)(2,1)}) %all-reduce.10.cloned.1.call-update) | async-done | bytes 262160 | tf_op jit(solution)/shard_map/psum | solution.py:12
  484.3 94.2 %reduce-scatter.11.cloned.1.call-done = f32[32,256]{1,0:T(8,128)} async-done(((f32[512,256]{1,0:T(8,128)}), f32[32,256]{1,0:T(8,128)}) %reduce-scatter.11.cloned.1.call-update) | async-done | bytes 32784 | tf_op jit(solution)/shard_map/reduce_scatter | solution.py:50
  579.3 11.7 all_to_all.41
  591.9 169.1 %all-reduce.12.cloned.1.call-done = bf16[512,256]{1,0:T(8,128)(2,1)} async-done(((bf16[512,256]{1,0:T(8,128)(2,1)}), bf16[512,256]{1,0:T(8,128)(2,1)}) %all-reduce.12.cloned.1.call-update) | async-done | bytes 262160 | tf_op jit(solution)/shard_map/psum | solution.py:12
  763.1 94.2 %reduce-scatter.13.cloned.1.call-done = f32[32,256]{1,0:T(8,128)} async-done(((f32[512,256]{1,0:T(8,128)}), f32[32,256]{1,0:T(8,128)}) %reduce-scatter.13.cloned.1.call-update) | async-done | bytes 32784 | tf_op jit(solution)/shard_map/reduce_scatter | solution.py:50
  858.2 11.7 all_to_all.42
  870.7 169.1 %all-reduce.14.cloned.1.call-done = bf16[512,256]{1,0:T(8,128)(2,1)} async-done(((bf16[512,256]{1,0:T(8,128)(2,1)}), bf16[512,256]{1,0:T(8,128)(2,1)}) %all-reduce.14.cloned.1.call-update) | async-done | bytes 262160 | tf_op jit(solution)/shard_map/psum | solution.py:12
  1042.0 94.4 %reduce-scatter.15.cloned.1.call-done = f32[32,256]{1,0:T(8,128)} async-done(((f32[512,256]{1,0:T(8,128)}), f32[32,256]{1,0:T(8,128)}) %reduce-scatter.15.cloned.1.call-update) | async-done | bytes 32784 | tf_op jit(solution)/shard_map/reduce_scatter | solution.py:50
  1137.1 11.7 all_to_all.43
  1149.7 169.1 %all-reduce.16.cloned.1.call-done = bf16[512,256]{1,0:T(8,128)(2,1)} async-done(((bf16[512,256]{1,0:T(8,128)(2,1)}), bf16[512,256]{1,0:T(8,128)(2,1)}) %all-reduce.16.cloned.1.call-update) | async-done | bytes 262160 | tf_op jit(solution)/shard_map/psum | solution.py:12
  1321.0 94.2 %reduce-scatter.17.cloned.1.call-done = f32[32,256]{1,0:T(8,128)} async-done(((f32[512,256]{1,0:T(8,128)}), f32[32,256]{1,0:T(8,128)}) %reduce-scatter.17.cloned.1.call-update) | async-done | bytes 32784 | tf_op jit(solution)/shard_map/reduce_scatter | solution.py:50
  1416.0 11.7 all_to_all.44
  1428.5 169.1 %all-reduce.18.cloned.1.call-done = bf16[512,256]{1,0:T(8,128)(2,1)} async-done(((bf16[512,256]{1,0:T(8,128)(2,1)}), bf16[512,256]{1,0:T(8,128)(2,1)}) %all-reduce.18.cloned.1.call-update) | async-done | bytes 262160 | tf_op jit(solution)/shard_map/psum | solution.py:12
  1599.8 94.2 %reduce-scatter.19.cloned.1.call-done = f32[32,256]{1,0:T(8,128)} async-done(((f32[512,256]{1,0:T(8,128)}), f32[32,256]{1,0:T(8,128)}) %reduce-scatter.19.cloned.1.call-update) | async-done | bytes 32784 | tf_op jit(solution)/shard_map/reduce_scatter | solution.py:50
  1694.8 11.7 all_to_all.45
  1707.4 169.1 %all-reduce.20.cloned.1.call-done = bf16[512,256]{1,0:T(8,128)(2,1)} async-done(((bf16[512,256]{1,0:T(8,128)(2,1)}), bf16[512,256]{1,0:T(8,128)(2,1)}) %all-reduce.20.cloned.1.call-update) | async-done | bytes 262160 | tf_op jit(solution)/shard_map/psum | solution.py:12
  1878.6 94.2 %reduce-scatter.21.cloned.1.call-done = f32[32,256]{1,0:T(8,128)} async-done(((f32[512,256]{1,0:T(8,128)}), f32[32,256]{1,0:T(8,128)}) %reduce-scatter.21.cloned.1.call-update) | async-done | bytes 32784 | tf_op jit(solution)/shard_map/reduce_scatter | solution.py:50
  1973.7 11.7 all_to_all.46
  1986.2 169.1 %all-reduce.22.cloned.1.call-done = bf16[512,256]{1,0:T(8,128)(2,1)} async-done(((bf16[512,256]{1,0:T(8,128)(2,1)}), bf16[512,256]{1,0:T(8,128)(2,1)}) %all-reduce.22.cloned.1.call-update) | async-done | bytes 262160 | tf_op jit(solution)/shard_map/psum | solution.py:12
  2157.4 94.2 %reduce-scatter.23.cloned.1.call-done = f32[32,256]{1,0:T(8,128)} async-done(((f32[512,256]{1,0:T(8,128)}), f32[32,256]{1,0:T(8,128)}) %reduce-scatter.23.cloned.1.call-update) | async-done | bytes 32784 | tf_op jit(solution)/shard_map/reduce_scatter | solution.py:50
  (89 shorter events, 44.0 us)
Async XLA Ops:
  6.5 10.1 copy-start
  8.1 19.4 all-to-all-start
  16.6 184.1 %all-reduce.24.cloned.1.call-start = ((), (), s32[]{:S(2)}) async-start(), calls=%async_computation.31 | async-start | bytes 2621440 | tf_op jit(solution)/shard_map/psum | solution.py:12
  28.2 172.5 %copy-start.1 = (bf16[2,512,256]{2,1,0:T(8,128)(2,1)S(1)}, bf16[2,512,256]{2,1,0:T(8,128)(2,1)}, u32[]{:S(2)}) copy-start(bf16[2,512,256]{2,1,0:T(8,128)(2,1)} %param.3) | copy-start | bytes 1572868
  28.2 271.5 %reduce-scatter.9.cloned.1.call-start = ((), (), s32[]{:S(2)}) async-start(), calls=%async_computation.16 | async-start | bytes 557056 | tf_op jit(solution)/shard_map/reduce_scatter | solution.py:50
  200.7 1.4 copy-start.3
  205.5 276.6 %all-reduce.10.cloned.1.call-start = ((), (), s32[]{:S(2)}) async-start(), calls=%async_computation.17 | async-start | bytes 524288 | tf_op jit(solution)/shard_map/psum | solution.py:12
  313.0 265.5 %reduce-scatter.11.cloned.1.call-start = ((), (), s32[]{:S(2)}) async-start(), calls=%async_computation.18 | async-start | bytes 557056 | tf_op jit(solution)/shard_map/reduce_scatter | solution.py:50
  484.3 276.7 %all-reduce.12.cloned.1.call-start = ((), (), s32[]{:S(2)}) async-start(), calls=%async_computation.19 | async-start | bytes 524288 | tf_op jit(solution)/shard_map/psum | solution.py:12
  591.8 265.6 %reduce-scatter.13.cloned.1.call-start = ((), (), s32[]{:S(2)}) async-start(), calls=%async_computation.20 | async-start | bytes 557056 | tf_op jit(solution)/shard_map/reduce_scatter | solution.py:50
  763.1 94.3 %copy-start.7 = (f32[32,256]{1,0:T(8,128)S(1)}, f32[32,256]{1,0:T(8,128)}, u32[]{:S(2)}) copy-start(f32[32,256]{1,0:T(8,128)} %reduce-scatter.11.cloned.1.call-done) | copy-start | bytes 98308
  763.1 276.7 %all-reduce.14.cloned.1.call-start = ((), (), s32[]{:S(2)}) async-start(), calls=%async_computation.21 | async-start | bytes 524288 | tf_op jit(solution)/shard_map/psum | solution.py:12
  870.7 265.7 %reduce-scatter.15.cloned.1.call-start = ((), (), s32[]{:S(2)}) async-start(), calls=%async_computation.22 | async-start | bytes 557056 | tf_op jit(solution)/shard_map/reduce_scatter | solution.py:50
  1041.9 276.9 %all-reduce.16.cloned.1.call-start = ((), (), s32[]{:S(2)}) async-start(), calls=%async_computation.23 | async-start | bytes 524288 | tf_op jit(solution)/shard_map/psum | solution.py:12
  1149.6 265.6 %reduce-scatter.17.cloned.1.call-start = ((), (), s32[]{:S(2)}) async-start(), calls=%async_computation.24 | async-start | bytes 557056 | tf_op jit(solution)/shard_map/reduce_scatter | solution.py:50
  1320.9 94.3 %copy-start.8 = (f32[32,256]{1,0:T(8,128)S(1)}, f32[32,256]{1,0:T(8,128)}, u32[]{:S(2)}) copy-start(f32[32,256]{1,0:T(8,128)} %reduce-scatter.15.cloned.1.call-done) | copy-start | bytes 98308
  1320.9 276.7 %all-reduce.18.cloned.1.call-start = ((), (), s32[]{:S(2)}) async-start(), calls=%async_computation.25 | async-start | bytes 524288 | tf_op jit(solution)/shard_map/psum | solution.py:12
  1428.5 265.6 %reduce-scatter.19.cloned.1.call-start = ((), (), s32[]{:S(2)}) async-start(), calls=%async_computation.26 | async-start | bytes 557056 | tf_op jit(solution)/shard_map/reduce_scatter | solution.py:50
  1599.8 276.7 %all-reduce.20.cloned.1.call-start = ((), (), s32[]{:S(2)}) async-start(), calls=%async_computation.27 | async-start | bytes 524288 | tf_op jit(solution)/shard_map/psum | solution.py:12
  1707.3 265.6 %reduce-scatter.21.cloned.1.call-start = ((), (), s32[]{:S(2)}) async-start(), calls=%async_computation.28 | async-start | bytes 557056 | tf_op jit(solution)/shard_map/reduce_scatter | solution.py:50
  1878.6 94.3 %copy-start.4 = (f32[32,256]{1,0:T(8,128)S(1)}, f32[32,256]{1,0:T(8,128)}, u32[]{:S(2)}) copy-start(f32[32,256]{1,0:T(8,128)} %reduce-scatter.19.cloned.1.call-done) | copy-start | bytes 98308
  1878.6 276.7 %all-reduce.22.cloned.1.call-start = ((), (), s32[]{:S(2)}) async-start(), calls=%async_computation.29 | async-start | bytes 524288 | tf_op jit(solution)/shard_map/psum | solution.py:12
  1986.2 265.5 %reduce-scatter.23.cloned.1.call-start = ((), (), s32[]{:S(2)}) async-start(), calls=%async_computation.30 | async-start | bytes 557056 | tf_op jit(solution)/shard_map/reduce_scatter | solution.py:50
  2157.4 94.2 %copy-start.6 = (f32[32,256]{1,0:T(8,128)S(1)}, f32[32,256]{1,0:T(8,128)}, u32[]{:S(2)}) copy-start(f32[32,256]{1,0:T(8,128)} %reduce-scatter.21.cloned.1.call-done) | copy-start | bytes 98308
  (2 other events, 2.0 us)
Sparse Core Ops, SparseCore 0:
  28.3 172.2 all-reduce.23
  205.7 94.0 reduce-scatter.8
  313.1 168.9 all-reduce.9
  484.5 93.9 reduce-scatter.10
  591.9 169.0 all-reduce.11
  763.3 93.9 reduce-scatter.12
  870.8 169.0 all-reduce.13
  1042.3 93.9 reduce-scatter.14
  1149.7 169.0 all-reduce.15
  1321.1 93.9 reduce-scatter.16
  1428.6 169.0 all-reduce.17
  1600.0 93.9 reduce-scatter.18
  1707.4 169.0 all-reduce.19
  1878.8 93.9 reduce-scatter.20
  1986.3 169.0 all-reduce.21
  2157.7 93.9 reduce-scatter.22
